TPU v7x, 32 devices: a whole 2x2x4 slice. The times are simulated.
32 devices in a mesh: dp: 2 (over x), ind: 4 (over z), probe: 4 (over y, core).
Axes of the slice: x: 2, y: 2, z: 4, core: 2. Of those that a mesh axis runs over, the one named last changes fastest.
Arguments:
- data_x: bfloat16 [16, 1024], P(None, 'dp'), may hold values from -6 to 6
- inducing_z: bfloat16 [16, 65536], P(None, 'ind'), may hold values from -6 to 6
- lengthscale: float32 [16], replicated, may hold values from 1.5 to 3
- noise_var: float32 [1], replicated, may hold values from 0.5 to 2
- solves: bfloat16 [32, 65536], P('probe', 'ind'), may hold values from -0.09375 to 0.09375
- probe_signs: int32 [32, 65536], P('probe', 'ind'), may hold values 0 or 1
Outputs:
- grad_z: float32 [16, 65536], P(None, 'ind')
All inputs are finite; a program needn't handle non-finite values. No bound on the sum of `probe_signs` on one device may be relied on, other than what follows from the above.
Results may differ from a plain program's by a relative error of at most 0.0095.
Values may be sent and summed in bfloat16 or wider, within the bound.
No kernel may reach another device: no remote copies, remote signals or barrier semaphores. Data moves between devices by JAX's collectives and lax.ppermute only.
A program may use at most 64 MiB of HBM per device.

v0:
```python
import jax
import jax.numpy as jnp
from jax import lax
from jax.sharding import PartitionSpec as P

P_SIZE = 32


def kernel_block(x_scaled, x_square, z_scaled, z_square):
    cross = lax.dot_general(
        x_scaled, z_scaled, (((0,), (0,)), ((), ())), preferred_element_type=jnp.float32
    )
    dist = x_square[:, None] + z_square[None, :] - 2.0 * cross
    return jnp.exp(-0.5 * dist).astype(jnp.bfloat16)


def on_device(data_x, inducing_z, lengthscale, noise_var, solves, probe_signs):
    probe_vals = (2 * probe_signs - 1).astype(jnp.bfloat16)
    stacked = jnp.concatenate([solves, probe_vals], axis=0)
    half_rows = stacked.shape[0] // 2
    inverse = 1.0 / lengthscale
    x_scaled = (data_x.astype(jnp.float32) * inverse[:, None]).astype(jnp.bfloat16)
    z_scaled = (inducing_z.astype(jnp.float32) * inverse[:, None]).astype(jnp.bfloat16)
    x_wide = x_scaled.astype(jnp.float32)
    z_wide = z_scaled.astype(jnp.float32)
    x_square = jnp.sum(x_wide * x_wide, axis=0)
    z_square = jnp.sum(z_wide * z_wide, axis=0)
    total_cols = z_scaled.shape[1]
    block_cols = min(2048, total_cols)
    blocks_count = total_cols // block_cols
    rows_count = x_scaled.shape[1]

    def first_pass(col_index, totals):
        start = col_index * block_cols
        z_part = lax.dynamic_slice_in_dim(z_scaled, start, block_cols, 1)
        zsq_part = lax.dynamic_slice_in_dim(z_square, start, block_cols, 0)
        kern = kernel_block(x_scaled, x_square, z_part, zsq_part)
        stack_part = lax.dynamic_slice_in_dim(stacked, start, block_cols, 1)
        return totals + lax.dot_general(
            stack_part, kern, (((1,), (1,)), ((), ())), preferred_element_type=jnp.float32
        )

    partial_proj = lax.fori_loop(
        0, blocks_count, first_pass, jnp.zeros((2 * half_rows, rows_count), jnp.float32)
    )
    projections = lax.psum(partial_proj.astype(jnp.bfloat16), "ind")
    swapped = jnp.concatenate([projections[half_rows:], projections[:half_rows]], axis=0)

    def second_pass(col_index, result):
        start = col_index * block_cols
        z_part = lax.dynamic_slice_in_dim(z_scaled, start, block_cols, 1)
        zsq_part = lax.dynamic_slice_in_dim(z_square, start, block_cols, 0)
        kern = kernel_block(x_scaled, x_square, z_part, zsq_part)
        stack_part = lax.dynamic_slice_in_dim(stacked, start, block_cols, 1)
        coef = lax.dot_general(
            swapped, stack_part, (((0,), (0,)), ((), ())), preferred_element_type=jnp.float32
        )
        weighted = (kern.astype(jnp.float32) * coef).astype(jnp.bfloat16)
        moment = jnp.dot(data_x, weighted, preferred_element_type=jnp.float32)
        row_total = jnp.sum(weighted, axis=0, dtype=jnp.float32)
        z_raw = lax.dynamic_slice_in_dim(inducing_z, start, block_cols, 1).astype(jnp.float32)
        return lax.dynamic_update_slice_in_dim(
            result, moment - z_raw * row_total[None, :], start, 1
        )

    partial_grad = lax.fori_loop(
        0, blocks_count, second_pass, jnp.zeros((x_scaled.shape[0], total_cols), jnp.float32)
    )
    summed = lax.psum(partial_grad, ("dp", "probe"))
    factor = inverse * inverse / (noise_var[0] * P_SIZE)
    return summed * factor[:, None]


def solution(mesh):
    return jax.shard_map(
        on_device,
        mesh=mesh,
        in_specs=(P(None, "dp"), P(None, "ind"), P(), P(), P("probe", "ind"), P("probe", "ind")),
        out_specs=P(None, "ind"),
        check_vma=False,
    )
```

profile of v0, /device:TPU:0, one launch (start us, length us, event | category | flops | bytes accessed | tf_op | source)
XLA Modules:
  0.0 134.0 jit_solution(3839862775014209474)
XLA Ops:
  6.5 0.0 copy-start.2
  6.5 0.0 all-reduce.2.cloned.1.call-start
  7.2 1.1 add_convert_fusion
  8.3 0.7 multiply_divide_fusion
  9.0 0.8 multiply_reduce_fusion.1
  9.8 1.4 %multiply_reduce_fusion = (f32[16384]{0:T(1024)S(1)}, bf16[16,16384]{1,0:T(8,128)(2,1)S(1)}) fusion(f32[16]{0:T(128)S(1)} %get-tuple-element.359, bf16[16,16384]{1,0:T(8,128)(2,1)} %param.11), kind=kLoop, calls=%fused_computation.25 | loop fusion | flops 1556480 | bytes 1114176 | tf_op jit(solution)/shard_map/reduce_sum | solution.py:27
  11.2 0.0 copy-done.2
  11.3 0.0 copy-start.1
  11.3 11.8 %while.28 = (s32[]{:T(128)}, f32[16,512]{1,0:T(8,128)S(1)}, bf16[16,16384]{1,0:T(8,128)(2,1)S(1)}, f32[512]{0:T(512)S(1)}, f32[16384]{0:T(1024)S(1)}, /*index=5*...) while((s32[]{:T(128)}, f32[16,512]{1,0:T(8,128)S(1)}, ...), condition=%wide.region_3.0_spmd.clone, body=%wide.region_2.0_spmd.clone.sunk | while | flops 72368136 | bytes 241328 | solution.py:43
  11.3 1.5 %fusion.49 = f32[16,512]{1,0:T(8,128)S(1)} fusion(bf16[16,512]{1,0:T(8,128)(2,1)S(1)} %get-tuple-element.504, f32[2048]{0:T(1024)S(1)} %dynamic_slice.77, f32[512]{0:T(512)S(1)} %get-tuple-element.501, bf16[16,16384]{1,0:T(8,128)(2,1)S(1)} %get-tuple-element.503, s32[]{:T(128)S(6)} %select_n.24, bf16[16,16384]{1,0:T(8,128)(2,1)S(1)} %get-tuple-element.500, ...), kind=kOutput, calls=%fused_computation.19.clone.1 | convolution fusion | flops 72368128 | bytes 224768 | tf_op jit(solution)/shard_map/while/body/eval_jaxpr/dot_general | solution.py:39
  12.8 1.5 %fusion.49 = f32[16,512]{1,0:T(8,128)S(1)} fusion(bf16[16,512]{1,0:T(8,128)(2,1)S(1)} %get-tuple-element.504, f32[2048]{0:T(1024)S(1)} %dynamic_slice.77, f32[512]{0:T(512)S(1)} %get-tuple-element.501, bf16[16,16384]{1,0:T(8,128)(2,1)S(1)} %get-tuple-element.503, s32[]{:T(128)S(6)} %select_n.24, bf16[16,16384]{1,0:T(8,128)(2,1)S(1)} %get-tuple-element.500, ...), kind=kOutput, calls=%fused_computation.19.clone.1 | convolution fusion | flops 72368128 | bytes 224768 | tf_op jit(solution)/shard_map/while/body/eval_jaxpr/dot_general | solution.py:39
  14.2 1.5 %fusion.49 = f32[16,512]{1,0:T(8,128)S(1)} fusion(bf16[16,512]{1,0:T(8,128)(2,1)S(1)} %get-tuple-element.504, f32[2048]{0:T(1024)S(1)} %dynamic_slice.77, f32[512]{0:T(512)S(1)} %get-tuple-element.501, bf16[16,16384]{1,0:T(8,128)(2,1)S(1)} %get-tuple-element.503, s32[]{:T(128)S(6)} %select_n.24, bf16[16,16384]{1,0:T(8,128)(2,1)S(1)} %get-tuple-element.500, ...), kind=kOutput, calls=%fused_computation.19.clone.1 | convolution fusion | flops 72368128 | bytes 224768 | tf_op jit(solution)/shard_map/while/body/eval_jaxpr/dot_general | solution.py:39
  15.7 1.5 %fusion.49 = f32[16,512]{1,0:T(8,128)S(1)} fusion(bf16[16,512]{1,0:T(8,128)(2,1)S(1)} %get-tuple-element.504, f32[2048]{0:T(1024)S(1)} %dynamic_slice.77, f32[512]{0:T(512)S(1)} %get-tuple-element.501, bf16[16,16384]{1,0:T(8,128)(2,1)S(1)} %get-tuple-element.503, s32[]{:T(128)S(6)} %select_n.24, bf16[16,16384]{1,0:T(8,128)(2,1)S(1)} %get-tuple-element.500, ...), kind=kOutput, calls=%fused_computation.19.clone.1 | convolution fusion | flops 72368128 | bytes 224768 | tf_op jit(solution)/shard_map/while/body/eval_jaxpr/dot_general | solution.py:39
  17.2 1.5 %fusion.49 = f32[16,512]{1,0:T(8,128)S(1)} fusion(bf16[16,512]{1,0:T(8,128)(2,1)S(1)} %get-tuple-element.504, f32[2048]{0:T(1024)S(1)} %dynamic_slice.77, f32[512]{0:T(512)S(1)} %get-tuple-element.501, bf16[16,16384]{1,0:T(8,128)(2,1)S(1)} %get-tuple-element.503, s32[]{:T(128)S(6)} %select_n.24, bf16[16,16384]{1,0:T(8,128)(2,1)S(1)} %get-tuple-element.500, ...), kind=kOutput, calls=%fused_computation.19.clone.1 | convolution fusion | flops 72368128 | bytes 224768 | tf_op jit(solution)/shard_map/while/body/eval_jaxpr/dot_general | solution.py:39
  18.7 1.5 %fusion.49 = f32[16,512]{1,0:T(8,128)S(1)} fusion(bf16[16,512]{1,0:T(8,128)(2,1)S(1)} %get-tuple-element.504, f32[2048]{0:T(1024)S(1)} %dynamic_slice.77, f32[512]{0:T(512)S(1)} %get-tuple-element.501, bf16[16,16384]{1,0:T(8,128)(2,1)S(1)} %get-tuple-element.503, s32[]{:T(128)S(6)} %select_n.24, bf16[16,16384]{1,0:T(8,128)(2,1)S(1)} %get-tuple-element.500, ...), kind=kOutput, calls=%fused_computation.19.clone.1 | convolution fusion | flops 72368128 | bytes 224768 | tf_op jit(solution)/shard_map/while/body/eval_jaxpr/dot_general | solution.py:39
  20.1 1.5 %fusion.49 = f32[16,512]{1,0:T(8,128)S(1)} fusion(bf16[16,512]{1,0:T(8,128)(2,1)S(1)} %get-tuple-element.504, f32[2048]{0:T(1024)S(1)} %dynamic_slice.77, f32[512]{0:T(512)S(1)} %get-tuple-element.501, bf16[16,16384]{1,0:T(8,128)(2,1)S(1)} %get-tuple-element.503, s32[]{:T(128)S(6)} %select_n.24, bf16[16,16384]{1,0:T(8,128)(2,1)S(1)} %get-tuple-element.500, ...), kind=kOutput, calls=%fused_computation.19.clone.1 | convolution fusion | flops 72368128 | bytes 224768 | tf_op jit(solution)/shard_map/while/body/eval_jaxpr/dot_general | solution.py:39
  21.6 1.5 %fusion.49 = f32[16,512]{1,0:T(8,128)S(1)} fusion(bf16[16,512]{1,0:T(8,128)(2,1)S(1)} %get-tuple-element.504, f32[2048]{0:T(1024)S(1)} %dynamic_slice.77, f32[512]{0:T(512)S(1)} %get-tuple-element.501, bf16[16,16384]{1,0:T(8,128)(2,1)S(1)} %get-tuple-element.503, s32[]{:T(128)S(6)} %select_n.24, bf16[16,16384]{1,0:T(8,128)(2,1)S(1)} %get-tuple-element.500, ...), kind=kOutput, calls=%fused_computation.19.clone.1 | convolution fusion | flops 72368128 | bytes 224768 | tf_op jit(solution)/shard_map/while/body/eval_jaxpr/dot_general | solution.py:39
  23.1 20.5 %psum.14 = bf16[16,512]{1,0:T(8,128)(2,1)S(1)} all-reduce(bf16[16,512]{1,0:T(8,128)(2,1)S(1)} %convert_element_type.73), channel_id=1, replica_groups=mesh['dp'=2,'ind'=4,'probe'=4] {'ind'}, use_global_device_ids=true, to_apply=%region_4.0 | all-reduce | flops 8192 | bytes 32768 | tf_op jit(solution)/shard_map/psum | solution.py:46
  43.6 0.1 broadcast_in_dim.24
  43.7 0.0 copy-done.1
  43.7 25.0 %while.27 = (s32[]{:T(128)}, f32[16,16384]{1,0:T(8,128)S(1)}, f32[512]{0:T(512)S(1)}, f32[16384]{0:T(1024)S(1)}, bf16[16,16384]{1,0:T(8,128)(2,1)S(1)}, /*index=...) while((s32[]{:T(128)}, f32[16,16384]{1,0:T(8,128)S(1)}, ...), condition=%wide.region_7.0_spmd, body=%wide.region_5.0_spmd.sunk | while | flops 111245312 | bytes 8808643 | solution.py:66
  43.8 1.1 fusion.44
  44.9 0.8 convert_reduce_fusion.2
  45.6 1.2 fusion.45
  46.9 1.1 fusion.44
  48.0 0.8 convert_reduce_fusion.2
  48.8 1.2 fusion.45
  50.0 1.1 fusion.44
  51.1 0.8 convert_reduce_fusion.2
  51.9 1.2 fusion.45
  53.1 1.1 fusion.44
  54.2 0.8 convert_reduce_fusion.2
  55.0 1.2 fusion.45
  56.2 1.1 fusion.44
  57.4 0.8 convert_reduce_fusion.2
  58.1 1.2 fusion.45
  59.4 1.1 fusion.44
  60.5 0.8 convert_reduce_fusion.2
  61.2 1.2 fusion.45
  62.5 1.1 fusion.44
  63.6 0.8 convert_reduce_fusion.2
  64.4 1.2 fusion.45
  65.6 1.1 fusion.44
  66.7 0.8 convert_reduce_fusion.2
  67.5 1.2 fusion.45
  68.7 0.0 copy-start
  68.7 1.0 copy-done
  69.7 0.0 all-reduce.2.cloned.1.call-update
  69.7 55.1 %all-reduce.2.cloned.1.call-done = f32[16,16384]{1,0:T(8,128)} async-done(((f32[16,16384]{1,0:T(8,128)}), f32[16,16384]{1,0:T(8,128)}) %all-reduce.2.cloned.1.call-update) | async-done | bytes 1048592 | tf_op jit(solution)/shard_map/psum | solution.py:69
  124.8 2.3 %broadcast_multiply_fusion = f32[16,16384]{1,0:T(8,128)} fusion(f32[16,16384]{1,0:T(8,128)} %all-reduce.2.cloned.1.call-done, f32[16]{0:T(128)S(1)} %get-tuple-element.358), kind=kLoop, calls=%fused_computation.28 | loop fusion | flops 262144 | bytes 2097216 | tf_op jit(solution)/shard_map/mul | solution.py:71
  (21 shorter events, 0.1 us)
Async XLA Ops:
  6.5 4.7 %copy-start.2 = (bf16[8,16384]{1,0:T(8,128)(2,1)S(1)}, bf16[8,16384]{1,0:T(8,128)(2,1)}, u32[]{:S(2)}) copy-start(bf16[8,16384]{1,0:T(8,128)(2,1)} %param.14) | copy-start | bytes 786436
  6.5 118.3 %all-reduce.2.cloned.1.call-start = ((), (), s32[]{:S(2)}) async-start(), calls=%async_computation | async-start | bytes 2097152 | tf_op jit(solution)/shard_map/psum | solution.py:69
  11.3 32.4 %copy-start.1 = (bf16[16,512]{1,0:T(8,128)(2,1)S(1)}, bf16[16,512]{1,0:T(8,128)(2,1)}, u32[]{:S(2)}) copy-start(bf16[16,512]{1,0:T(8,128)(2,1)} %param.10) | copy-start | bytes 49156
  68.7 1.0 copy-start
Sparse Core Ops, SparseCore 0:
  69.9 54.8 all-reduce.1
where the time goes:
time: 135 us; the launch traced here: 134 us
  waiting for transfers between devices  55.1 us (41%)
  matrix products  36.6 us (27%)
  blocking collectives  20.5 us (15%)
  between operations  14.1 us (10%)
  other arithmetic  6.35 us (5%)
    psum x1, waiting for transfers between devices, on_device(): summed = lax.psum(partial_grad, ('dp', 'probe'))  55.1 us
    psum x1, blocking collectives, on_device(): projections = lax.psum(partial_proj.astype(jnp.bfloat16), 'ind')  20.5 us
    dot_general x8, matrix products, first_pass(): lax.dot_general(stack_part, kern, (((1,), (1,)), ((), ())), preferred_ele...  11.8 us
    dot_general x8, matrix products, second_pass(): moment = jnp.dot(data_x, weighted, preferred_element_type=jnp.float32)  9.92 us
    dot_general x8, matrix products, kernel_block(): lax.dot_general(x_scaled, z_scaled, (((0,), (0,)), ((), ())), preferred_e...  8.83 us
    dot_general x8, matrix products, second_pass(): lax.dot_general(swapped, stack_part, (((0,), (0,)), ((), ())), preferred_...  6.1 us
  transfers between devices with their start and end apart: 1, of which 1 were waited for; matrix products, arithmetic and copies ran while one was open for 0% of the time, Pallas kernels for 0%

commit v1 on v0

--- a/solution.py
+++ b/solution.py
@@ -66,7 +66,8 @@
     partial_grad = lax.fori_loop(
         0, blocks_count, second_pass, jnp.zeros((x_scaled.shape[0], total_cols), jnp.float32)
     )
-    summed = lax.psum(partial_grad, ("dp", "probe"))
+    inner = lax.psum(partial_grad, "probe")
+    summed = lax.psum(inner, "dp")
     factor = inverse * inverse / (noise_var[0] * P_SIZE)
     return summed * factor[:, None]
 

time: 135 us -> 157 us (1.16)
  waiting for transfers between devices: 55.1 us -> 77.5 us
    psum x1 -> x2, waiting for transfers between devices: 55.1 us -> 77.5 us  [the longest x1 42.9 us: on_device(): summed = lax.psum(inner, 'dp')]
  transfers between devices with their start and end apart: 1 -> 2, of which waited for: 1 -> 2; matrix products, arithmetic and copies ran while one was open for 0% -> 0% of each run, Pallas kernels for 0% -> 0%
where the time goes in v1:
time: 157 us; the launch traced here: 156 us
  waiting for transfers between devices  77.5 us (49%)
  matrix products  36.6 us (23%)
  blocking collectives  20.5 us (13%)
  between operations  14.2 us (9%)
  other arithmetic  6.35 us (4%)
    psum x1, waiting for transfers between devices, on_device(): summed = lax.psum(inner, 'dp')  42.9 us
    psum x1, waiting for transfers between devices, on_device(): inner = lax.psum(partial_grad, 'probe')  34.6 us
    psum x1, blocking collectives, on_device(): projections = lax.psum(partial_proj.astype(jnp.bfloat16), 'ind')  20.5 us
    dot_general x8, matrix products, first_pass(): lax.dot_general(stack_part, kern, (((1,), (1,)), ((), ())), preferred_ele...  11.8 us
    dot_general x8, matrix products, second_pass(): moment = jnp.dot(data_x, weighted, preferred_element_type=jnp.float32)  9.92 us
    dot_general x8, matrix products, kernel_block(): lax.dot_general(x_scaled, z_scaled, (((0,), (0,)), ((), ())), preferred_e...  8.83 us
    dot_general x8, matrix products, second_pass(): lax.dot_general(swapped, stack_part, (((0,), (0,)), ((), ())), preferred_...  6.1 us
  transfers between devices with their start and end apart: 2, of which 2 were waited for; matrix products, arithmetic and copies ran while one was open for 0% of the time, Pallas kernels for 0%

profile of v1, /device:TPU:0, one launch (start us, length us, event | category | flops | bytes accessed | tf_op | source)
XLA Modules:
  0.0 156.4 jit_solution(9150705907351827267)
XLA Ops:
  6.5 0.0 copy-start.2
  6.5 0.0 all-reduce.3.cloned.1.call-start
  7.2 1.1 add_convert_fusion
  8.3 0.7 multiply_divide_fusion
  9.0 0.8 multiply_reduce_fusion.1
  9.8 1.4 multiply_reduce_fusion
  11.2 0.0 copy-done.2
  11.3 0.0 copy-start.1
  11.3 11.8 %while.28 = (s32[]{:T(128)}, f32[16,512]{1,0:T(8,128)S(1)}, bf16[16,16384]{1,0:T(8,128)(2,1)S(1)}, f32[512]{0:T(512)S(1)}, f32[16384]{0:T(1024)S(1)}, /*index=5*...) while((s32[]{:T(128)}, f32[16,512]{1,0:T(8,128)S(1)}, ...), condition=%wide.region_3.0_spmd.clone, body=%wide.region_2.0_spmd.clone.sunk | while | flops 72368136 | bytes 241328 | solution.py:43
  11.3 1.5 fusion.49
  12.8 1.5 fusion.49
  14.2 1.5 fusion.49
  15.7 1.5 fusion.49
  17.2 1.5 fusion.49
  18.7 1.5 fusion.49
  20.1 1.5 fusion.49
  21.6 1.5 fusion.49
  23.1 20.5 %psum.21 = bf16[16,512]{1,0:T(8,128)(2,1)S(1)} all-reduce(bf16[16,512]{1,0:T(8,128)(2,1)S(1)} %convert_element_type.73), channel_id=1, replica_groups=mesh['dp'=2,'ind'=4,'probe'=4] {'ind'}, use_global_device_ids=true, to_apply=%region_4.0 | all-reduce | flops 8192 | bytes 32768 | tf_op jit(solution)/shard_map/psum | solution.py:46
  43.6 0.1 broadcast_in_dim.24
  43.7 0.0 copy-done.1
  43.7 25.0 %while.27 = (s32[]{:T(128)}, f32[16,16384]{1,0:T(8,128)S(1)}, f32[512]{0:T(512)S(1)}, f32[16384]{0:T(1024)S(1)}, bf16[16,16384]{1,0:T(8,128)(2,1)S(1)}, /*index=...) while((s32[]{:T(128)}, f32[16,16384]{1,0:T(8,128)S(1)}, ...), condition=%wide.region_7.0_spmd, body=%wide.region_5.0_spmd.sunk | while | flops 111245312 | bytes 8808643 | solution.py:66
  43.8 1.1 fusion.44
  44.9 0.8 convert_reduce_fusion.2
  45.6 1.2 fusion.45
  46.9 1.1 fusion.44
  48.0 0.8 convert_reduce_fusion.2
  48.8 1.2 fusion.45
  50.0 1.1 fusion.44
  51.1 0.8 convert_reduce_fusion.2
  51.9 1.2 fusion.45
  53.1 1.1 fusion.44
  54.2 0.8 convert_reduce_fusion.2
  55.0 1.2 fusion.45
  56.2 1.1 fusion.44
  57.4 0.8 convert_reduce_fusion.2
  58.1 1.2 fusion.45
  59.4 1.1 fusion.44
  60.5 0.8 convert_reduce_fusion.2
  61.2 1.2 fusion.45
  62.5 1.1 fusion.44
  63.6 0.8 convert_reduce_fusion.2
  64.4 1.2 fusion.45
  65.6 1.1 fusion.44
  66.7 0.8 convert_reduce_fusion.2
  67.5 1.2 fusion.45
  68.7 0.0 copy-start
  68.7 1.0 copy-done
  69.7 0.0 all-reduce.3.cloned.1.call-update
  69.7 0.0 all-reduce.5.cloned.1.call-start
  69.8 34.6 %all-reduce.3.cloned.1.call-done = f32[16,16384]{1,0:T(8,128)} async-done(((f32[16,16384]{1,0:T(8,128)}), f32[16,16384]{1,0:T(8,128)}) %all-reduce.3.cloned.1.call-update) | async-done | bytes 1048592 | tf_op jit(solution)/shard_map/psum | solution.py:69
  104.4 0.0 all-reduce.5.cloned.1.call-update
  104.4 42.9 %all-reduce.5.cloned.1.call-done = f32[16,16384]{1,0:T(8,128)} async-done(((f32[16,16384]{1,0:T(8,128)}), f32[16,16384]{1,0:T(8,128)}) %all-reduce.5.cloned.1.call-update) | async-done | bytes 1048592 | tf_op jit(solution)/shard_map/psum | solution.py:70
  147.3 2.3 %broadcast_multiply_fusion = f32[16,16384]{1,0:T(8,128)} fusion(f32[16,16384]{1,0:T(8,128)} %all-reduce.5.cloned.1.call-done, f32[16]{0:T(128)S(1)} %get-tuple-element.358), kind=kLoop, calls=%fused_computation.28 | loop fusion | flops 262144 | bytes 2097216 | tf_op jit(solution)/shard_map/mul | solution.py:72
  (21 shorter events, 0.1 us)
Async XLA Ops:
  6.5 4.7 %copy-start.2 = (bf16[8,16384]{1,0:T(8,128)(2,1)S(1)}, bf16[8,16384]{1,0:T(8,128)(2,1)}, u32[]{:S(2)}) copy-start(bf16[8,16384]{1,0:T(8,128)(2,1)} %param.14) | copy-start | bytes 786436
  6.5 97.8 %all-reduce.3.cloned.1.call-start = ((), (), s32[]{:S(2)}) async-start(), calls=%async_computation | async-start | bytes 2097152 | tf_op jit(solution)/shard_map/psum | solution.py:69
  11.3 32.4 %copy-start.1 = (bf16[16,512]{1,0:T(8,128)(2,1)S(1)}, bf16[16,512]{1,0:T(8,128)(2,1)}, u32[]{:S(2)}) copy-start(bf16[16,512]{1,0:T(8,128)(2,1)} %param.10) | copy-start | bytes 49156
  68.7 1.0 copy-start
  69.7 77.5 %all-reduce.5.cloned.1.call-start = ((), (), s32[]{:S(2)}) async-start(), calls=%async_computation.1 | async-start | bytes 2097152 | tf_op jit(solution)/shard_map/psum | solution.py:70
Sparse Core Ops, SparseCore 0:
  69.9 34.4 all-reduce.2
  106.7 40.5 all-reduce.4
